TPU v7x, 32 devices: a whole 2x2x4 slice. The times are simulated.
32 devices in a mesh: wide: 16 (over z, y, x), narrow: 2 (over core).
Axes of the slice: x: 2, y: 2, z: 4, core: 2. Of those that a mesh axis runs over, the one named last changes fastest.
Arguments:
- pressure: float32 [128, 128, 512], P('wide', 'narrow'), may hold values from -6 to 6
Outputs:
- detail_one: float32 [7, 64, 64, 256], P(None, 'wide', 'narrow')
- detail_two: float32 [7, 32, 32, 128], P(None, 'wide', 'narrow')
- detail_three: float32 [7, 16, 16, 64], P(None, 'wide', 'narrow')
- bands_four: float32 [8, 8, 8, 32], P(None, None, 'narrow')
All inputs are finite; a program needn't handle non-finite values.
Results may differ from a plain program's by a relative error of at most 0.00016.
Values sent between devices are 32-bit elements; how exact they have to be, the bound alone decides.
No kernel may reach another device: no remote copies, remote signals or barrier semaphores. Data moves between devices by JAX's collectives and lax.ppermute only.
A program may use at most 64 MiB of HBM per device.

v0:
```python
import jax
import jax.numpy as jnp
from jax import lax
from jax.sharding import PartitionSpec as P

LEVELS = 4
LIFT_ALPHA = -1.586134342
LIFT_BETA = -0.05298011854
LIFT_GAMMA = 0.8829110762
LIFT_DELTA = 0.4435068522
LIFT_ZETA = 1.149604398
LIFT_INVERSE = 1.0 / 1.149604398


def extended(cells, sides, width):
    for axis, dim in sides:
        count = lax.axis_size(axis)
        ends = count - 1
        head = lax.slice_in_dim(cells, 0, width, axis=dim)
        tail = lax.slice_in_dim(cells, cells.shape[dim] - width, cells.shape[dim], axis=dim)
        cells = jnp.concatenate(
            [
                lax.ppermute(tail, axis, [(i, (i + 1) % count) for i in range(ends)]),
                cells,
                lax.ppermute(head, axis, [((i + 1) % count, i) for i in range(ends)]),
            ],
            axis=dim,
        )
    return cells


def shifted(value, axis, steps):
    count = lax.axis_size(axis)
    first, last = (max(0, -steps), min(count, count - steps))
    return lax.ppermute(value, axis, [(source, source + steps) for source in range(first, last)])


def keep_same(piece):
    return piece


def lift_general(volume, along, pull_next, pull_prev, at_first, at_last):
    length = volume.shape[along]
    half = length // 2
    even_part = lax.slice_in_dim(volume, 0, length, 2, along)
    odd_part = lax.slice_in_dim(volume, 1, length, 2, along)

    def next_even(source):
        edge = lax.slice_in_dim(source, half - 1, half, 1, along)
        outer = jnp.where(at_last, edge, pull_next(lax.slice_in_dim(source, 0, 1, 1, along)))
        return jnp.concatenate([lax.slice_in_dim(source, 1, half, 1, along), outer], along)

    def prev_odd(source):
        edge = lax.slice_in_dim(source, 0, 1, 1, along)
        outer = jnp.where(
            at_first, edge, pull_prev(lax.slice_in_dim(source, half - 1, half, 1, along))
        )
        return jnp.concatenate([outer, lax.slice_in_dim(source, 0, half - 1, 1, along)], along)

    odd_part = odd_part + LIFT_ALPHA * (even_part + next_even(even_part))
    even_part = even_part + LIFT_BETA * (prev_odd(odd_part) + odd_part)
    odd_part = odd_part + LIFT_GAMMA * (even_part + next_even(even_part))
    even_part = even_part + LIFT_DELTA * (prev_odd(odd_part) + odd_part)
    return jnp.stack([even_part * LIFT_ZETA, odd_part * LIFT_INVERSE], 0)


def lift_local(volume, along):
    return lift_general(volume, along, keep_same, keep_same, True, True)


def lift_columns(volume):
    width = volume.shape[2]
    unit_matrix = jnp.eye(width, dtype=jnp.float32)
    lift_table = lift_local(unit_matrix, 1)
    return jnp.einsum("zyi,bij->bzyj", volume, lift_table, precision=lax.Precision.HIGHEST)


def lift_widened(widened, along, at_first, at_last):
    total = widened.shape[along]
    left_mirror = jnp.flip(lax.slice_in_dim(widened, 5, 9, 1, along), along)
    right_mirror = jnp.flip(lax.slice_in_dim(widened, total - 9, total - 5, 1, along), along)
    left_part = jnp.where(at_first, left_mirror, lax.slice_in_dim(widened, 0, 4, 1, along))
    right_part = jnp.where(
        at_last, right_mirror, lax.slice_in_dim(widened, total - 4, total, 1, along)
    )
    middle = lax.slice_in_dim(widened, 4, total - 4, 1, along)
    filled = jnp.concatenate([left_part, middle, right_part], along)
    lifted = lift_local(filled, along)
    owned = (total - 8) // 2
    return lax.slice_in_dim(lifted, 2, 2 + owned, 1, along + 1)


def widen_rows(piece):
    return extended(piece, (("narrow", 2),), 4)


def widen_planes(piece):
    return extended(piece, (("wide", 2),), 4)


def pull_next_y(piece):
    return shifted(piece, "narrow", -1)


def pull_prev_y(piece):
    return shifted(piece, "narrow", 1)


def pull_next_z(piece):
    return shifted(piece, "wide", -1)


def pull_prev_z(piece):
    return shifted(piece, "wide", 1)


def per_device(pressure):
    wide_index = lax.axis_index("wide")
    narrow_index = lax.axis_index("narrow")
    wide_count = lax.axis_size("wide")
    wide_first = wide_index == 0
    wide_last = wide_index == wide_count - 1
    narrow_first = narrow_index == 0
    narrow_last = narrow_index == lax.axis_size("narrow") - 1
    volume = pressure
    details = []
    for _ in range(LEVELS - 1):
        planes_here = volume.shape[0]
        x_pair = lift_columns(volume)
        y_pair = lift_widened(widen_rows(x_pair), 2, narrow_first, narrow_last)
        if planes_here >= 4:
            z_pair = lift_widened(widen_planes(y_pair), 2, wide_first, wide_last)
        else:
            z_pair = lift_general(y_pair, 2, pull_next_z, pull_prev_z, wide_first, wide_last)
        band_set = z_pair.reshape((8,) + z_pair.shape[3:])
        details.append(band_set[1:])
        volume = band_set[0]
    whole = lax.all_gather(volume, "wide", axis=0, tiled=True)
    x_pair = lift_columns(whole)
    y_pair = lift_general(x_pair, 2, pull_next_y, pull_prev_y, narrow_first, narrow_last)
    z_pair = lift_local(y_pair, 2)
    last_bands = z_pair.reshape((8,) + z_pair.shape[3:])
    return (details[0], details[1], details[2], last_bands)


def solution(mesh):
    in_specs = (P("wide", "narrow", None),)
    out_specs = (
        P(None, "wide", "narrow", None),
        P(None, "wide", "narrow", None),
        P(None, "wide", "narrow", None),
        P(None, None, "narrow", None),
    )
    return jax.shard_map(
        per_device, mesh=mesh, in_specs=in_specs, out_specs=out_specs, check_vma=False
    )
```

profile of v0, /device:TPU:0, one launch (start us, length us, event | category | flops | bytes accessed | tf_op | source)
XLA Modules:
  0.0 196.4 jit_solution(12183372360742501875)
XLA Ops:
  0.8 19.5 %slice.508 = f32[512,256]{1,0:T(8,128)S(1)} slice(f32[512,512]{1,0:T(8,128)S(1)} %fusion.14), slice={[0:512:1], [1:512:2]} | slice | bytes 1048576 | tf_op jit(solution)/shard_map/slice | solution.py:46
  20.2 19.5 %slice.507 = f32[512,256]{1,0:T(8,128)S(1)} slice(f32[512,512]{1,0:T(8,128)S(1)} %fusion.14), slice={[0:512:1], [0:512:2]} | slice | bytes 1048576 | tf_op jit(solution)/shard_map/slice | solution.py:45
  41.2 1.9 convolution_bitcast_fusion
  43.1 1.3 collective-permute-start.1
  44.4 3.2 %collective-permute-start = (f32[2,8,4,256]{3,2,1,0:T(4,128)S(1)}, f32[2,8,4,256]{3,2,1,0:T(4,128)S(1)}, u32[]{:S(2)}, u32[]{:S(2)}) collective-permute-start(f32[2,8,4,256]{3,2,1,0:T(4,128)S(1)} %get-tuple-element.40), channel_id=1, source_target_pairs={{0,1},{2,3},{4,5},{6,7},{8,9},{10,11},{12,13},{14,15},{16,17},{18,... | collective-permute-start | bytes 196616 | tf_op jit(solution)/shard_map/ppermute | solution.py:23
  47.7 4.5 %slice.549 = f32[256,128]{1,0:T(8,128)S(1)} slice(f32[256,256]{1,0:T(8,128)S(1)} %fusion.40), slice={[0:256:1], [1:256:2]} | slice | bytes 262144 | tf_op jit(solution)/shard_map/slice | solution.py:46
  52.2 4.5 %slice.548 = f32[256,128]{1,0:T(8,128)S(1)} slice(f32[256,256]{1,0:T(8,128)S(1)} %fusion.40), slice={[0:256:1], [0:256:2]} | slice | bytes 262144 | tf_op jit(solution)/shard_map/slice | solution.py:45
  57.3 0.8 slice.693
  58.0 0.7 slice.692
  58.8 0.6 slice.722
  59.9 0.6 slice.521
  60.6 2.2 %slice.522 = f32[2,8,36,256]{3,2,1,0:T(8,128)} slice(f32[2,8,72,256]{3,2,1,0:T(8,128)S(1)} %pad_maximum_fusion.1), slice={[0:2:1], [0:8:1], [1:72:2], [0:256:1]} | slice | bytes 1179648 | tf_op jit(solution)/shard_map/slice | solution.py:46
  62.8 1.0 copy-done.1
  64.8 1.3 collective-permute-start.3
  66.2 5.5 %collective-permute-start.2 = (f32[2,2,4,32,256]{4,3,2,1,0:T(8,128)S(1)}, f32[2,2,4,32,256]{4,3,2,1,0:T(8,128)S(1)}, u32[]{:S(2)}, u32[]{:S(2)}) collective-permute-start(f32[2,2,4,32,256]{4,3,2,1,0:T(8,128)S(1)} %get-tuple-element.37), channel_id=1, source_target_pairs={{0,2},{2,4},{4,6},{6,8},{8,10},{10,12},{12,14},{14,16},{16,18},{18... | collective-permute-start | bytes 1572872 | tf_op jit(solution)/shard_map/ppermute | solution.py:23
  72.0 10.4 %collective-permute-done.3 = f32[2,2,4,32,256]{4,3,2,1,0:T(8,128)S(1)} collective-permute-done((f32[2,2,4,32,256]{4,3,2,1,0:T(8,128)S(1)}, f32[2,2,4,32,256]{4,3,2,1,0:T(8,128)S(1)}, u32[]{:S(2)}, u32[]{:S(2)}) %collective-permute-start.3) | collective-permute-done | bytes 524320 | tf_op jit(solution)/shard_map/ppermute | solution.py:25
  82.5 11.0 %collective-permute-done.2 = f32[2,2,4,32,256]{4,3,2,1,0:T(8,128)S(1)} collective-permute-done((f32[2,2,4,32,256]{4,3,2,1,0:T(8,128)S(1)}, f32[2,2,4,32,256]{4,3,2,1,0:T(8,128)S(1)}, u32[]{:S(2)}, u32[]{:S(2)}) %collective-permute-start.2) | collective-permute-done | bytes 524320 | tf_op jit(solution)/shard_map/ppermute | solution.py:23
  94.8 0.3 multiply_bitcast_fusion
  96.0 1.3 collective-permute-start.5
  97.4 3.0 %collective-permute-start.4 = (f32[2,4,4,128]{3,2,1,0:T(4,128)S(1)}, f32[2,4,4,128]{3,2,1,0:T(4,128)S(1)}, u32[]{:S(2)}, u32[]{:S(2)}) collective-permute-start(f32[2,4,4,128]{3,2,1,0:T(4,128)S(1)} %get-tuple-element.46), channel_id=1, source_target_pairs={{0,1},{2,3},{4,5},{6,7},{8,9},{10,11},{12,13},{14,15},{16,17},{18,... | collective-permute-start | bytes 49160 | tf_op jit(solution)/shard_map/ppermute | solution.py:23
  100.5 0.8 collective-permute-done.4
  101.8 1.3 collective-permute-start.6
  103.1 5.0 %collective-permute-start.7 = (f32[2,2,4,16,128]{4,3,2,1,0:T(8,128)S(1)}, f32[2,2,4,16,128]{4,3,2,1,0:T(8,128)S(1)}, u32[]{:S(2)}, u32[]{:S(2)}) collective-permute-start(f32[2,2,4,16,128]{4,3,2,1,0:T(8,128)S(1)} %pad_maximum_fusion.9), channel_id=1, source_target_pairs={{0,2},{2,4},{4,6},{6,8},{8,10},{10,12},{12,14},{14,16},{16,18},{18... | collective-permute-start | bytes 393224 | tf_op jit(solution)/shard_map/ppermute | solution.py:23
  108.1 2.0 %collective-permute-done.6 = f32[2,2,4,16,128]{4,3,2,1,0:T(8,128)S(1)} collective-permute-done((f32[2,2,4,16,128]{4,3,2,1,0:T(8,128)S(1)}, f32[2,2,4,16,128]{4,3,2,1,0:T(8,128)S(1)}, u32[]{:S(2)}, u32[]{:S(2)}) %collective-permute-start.6) | collective-permute-done | bytes 131104 | tf_op jit(solution)/shard_map/ppermute | solution.py:25
  110.2 2.0 %collective-permute-done.7 = f32[2,2,4,16,128]{4,3,2,1,0:T(8,128)S(1)} collective-permute-done((f32[2,2,4,16,128]{4,3,2,1,0:T(8,128)S(1)}, f32[2,2,4,16,128]{4,3,2,1,0:T(8,128)S(1)}, u32[]{:S(2)}, u32[]{:S(2)}) %collective-permute-start.7) | collective-permute-done | bytes 131104 | tf_op jit(solution)/shard_map/ppermute | solution.py:23
  113.0 1.3 collective-permute-start.9
  114.4 3.0 %collective-permute-start.8 = (f32[2,2,4,64]{3,2,1,0:T(4,128)S(1)}, f32[2,2,4,64]{3,2,1,0:T(4,128)S(1)}, u32[]{:S(2)}, u32[]{:S(2)}) collective-permute-start(f32[2,2,4,64]{3,2,1,0:T(4,128)S(1)} %get-tuple-element.50), channel_id=1, source_target_pairs={{0,1},{2,3},{4,5},{6,7},{8,9},{10,11},{12,13},{14,15},{16,17},{18,... | collective-permute-start | bytes 12296 | tf_op jit(solution)/shard_map/ppermute | solution.py:23
  117.5 0.8 collective-permute-done.8
  118.7 1.3 collective-permute-start.10
  120.0 4.7 %collective-permute-done.10 = f32[2,2,1,8,64]{4,3,1,0,2:T(8,128)S(1)} collective-permute-done((f32[2,2,1,8,64]{4,3,1,0,2:T(8,128)S(1)}, f32[2,2,1,8,64]{4,3,1,0,2:T(8,128)S(1)}, u32[]{:S(2)}, u32[]{:S(2)}) %collective-permute-start.10) | collective-permute-done | bytes 8224 | tf_op jit(solution)/shard_map/ppermute | solution.py:35
  124.7 4.8 %collective-permute-start.11 = (f32[2,2,1,8,64]{4,3,1,0,2:T(8,128)S(1)}, f32[2,2,1,8,64]{4,3,1,0,2:T(8,128)S(1)}, u32[]{:S(2)}, u32[]{:S(2)}) collective-permute-start(f32[2,2,1,8,64]{4,3,1,0,2:T(8,128)S(1)} %bitcast.179), channel_id=1, source_target_pairs={{0,2},{2,4},{4,6},{6,8},{8,10},{10,12},{12,14},{14,16},{16,18},{18... | collective-permute-start | bytes 24584 | tf_op jit(solution)/shard_map/ppermute | solution.py:35
  129.6 1.4 collective-permute-done.11
  131.0 1.3 collective-permute-start.12
  132.3 4.6 %collective-permute-done.12 = f32[2,2,1,8,64]{4,3,1,0,2:T(8,128)S(1)} collective-permute-done((f32[2,2,1,8,64]{4,3,1,0,2:T(8,128)S(1)}, f32[2,2,1,8,64]{4,3,1,0,2:T(8,128)S(1)}, u32[]{:S(2)}, u32[]{:S(2)}) %collective-permute-start.12) | collective-permute-done | bytes 8224 | tf_op jit(solution)/shard_map/ppermute | solution.py:35
  136.9 4.8 %collective-permute-start.13 = (f32[2,2,1,8,64]{4,3,1,0,2:T(8,128)S(1)}, f32[2,2,1,8,64]{4,3,1,0,2:T(8,128)S(1)}, u32[]{:S(2)}, u32[]{:S(2)}) collective-permute-start(f32[2,2,1,8,64]{4,3,1,0,2:T(8,128)S(1)} %bitcast.189), channel_id=1, source_target_pairs={{0,2},{2,4},{4,6},{6,8},{8,10},{10,12},{12,14},{14,16},{16,18},{18... | collective-permute-start | bytes 24584 | tf_op jit(solution)/shard_map/ppermute | solution.py:35
  141.8 1.4 collective-permute-done.13
  143.2 38.1 %all-gather = f32[16,1,8,64]{3,2,1,0:T(8,128)S(1)} all-gather(f32[1,1,8,64]{3,2,1,0:T(8,128)S(1)} %slice.748), channel_id=2, replica_groups=mesh['wide'=16,'narrow'=2] {'wide'}, dimensions={0}, use_global_device_ids=true | all-gather | bytes 34816 | tf_op jit(solution)/shard_map/all_gather | solution.py:138
  181.6 1.3 collective-permute-start.14
  183.0 1.8 collective-permute-done.14
  184.8 2.1 %collective-permute-start.15 = (f32[2,16,1,32]{3,1,2,0:T(8,128)S(1)}, f32[2,16,1,32]{3,1,2,0:T(8,128)S(1)}, u32[]{:S(2)}, u32[]{:S(2)}) collective-permute-start(f32[2,16,1,32]{3,1,2,0:T(8,128)S(1)} %slice.753), channel_id=1, source_target_pairs={{0,1},{2,3},{4,5},{6,7},{8,9},{10,11},{12,13},{14,15},{16,17},{18,... | collective-permute-start | bytes 12296 | tf_op jit(solution)/shard_map/ppermute | solution.py:35
  186.8 0.8 collective-permute-done.15
  187.7 1.3 collective-permute-start.16
  189.0 1.8 collective-permute-done.16
  190.8 2.1 %collective-permute-start.17 = (f32[2,16,1,32]{3,1,2,0:T(8,128)S(1)}, f32[2,16,1,32]{3,1,2,0:T(8,128)S(1)}, u32[]{:S(2)}, u32[]{:S(2)}) collective-permute-start(f32[2,16,1,32]{3,1,2,0:T(8,128)S(1)} %slice.759), channel_id=1, source_target_pairs={{0,1},{2,3},{4,5},{6,7},{8,9},{10,11},{12,13},{14,15},{16,17},{18,... | collective-permute-start | bytes 12296 | tf_op jit(solution)/shard_map/ppermute | solution.py:35
  192.9 1.0 slice.687
  193.9 0.7 slice.717
  194.5 0.6 slice.739
  195.7 0.7 copy.29
  (195 shorter events, 8.5 us)
Async XLA Ops:
  0.6 40.6 %copy-start = (f32[8,64,512]{2,1,0:T(8,128)S(1)}, f32[8,64,512]{2,1,0:T(8,128)}, u32[]{:S(2)}) copy-start(f32[8,64,512]{2,1,0:T(8,128)} %param.1) | copy-start | bytes 3145732
  43.1 16.5 %collective-permute-start.1 = (f32[2,8,4,256]{3,2,1,0:T(4,128)S(1)}, f32[2,8,4,256]{3,2,1,0:T(4,128)S(1)}, u32[]{:S(2)}, u32[]{:S(2)}) collective-permute-start(f32[2,8,4,256]{3,2,1,0:T(4,128)S(1)} %get-tuple-element.41), channel_id=1, source_target_pairs={{1,0},{3,2},{5,4},{7,6},{9,8},{11,10},{13,12},{15,14},{17,16},{19,... | collective-permute-start | bytes 196616 | tf_op jit(solution)/shard_map/ppermute | solution.py:25
  44.4 15.3 %collective-permute-start = (f32[2,8,4,256]{3,2,1,0:T(4,128)S(1)}, f32[2,8,4,256]{3,2,1,0:T(4,128)S(1)}, u32[]{:S(2)}, u32[]{:S(2)}) collective-permute-start(f32[2,8,4,256]{3,2,1,0:T(4,128)S(1)} %get-tuple-element.40), channel_id=1, source_target_pairs={{0,1},{2,3},{4,5},{6,7},{8,9},{10,11},{12,13},{14,15},{16,17},{18,... | collective-permute-start | bytes 196616 | tf_op jit(solution)/shard_map/ppermute | solution.py:23
  57.0 2.8 %copy-start.6 = (f32[128,64]{0,1:T(8,128)}, f32[128,64]{0,1:T(8,128)S(1)}, u32[]{:S(2)}) copy-start(f32[128,64]{0,1:T(8,128)S(1)} %fusion.97) | copy-start | bytes 98308
  57.3 2.5 %copy-start.2 = (f32[128,64]{0,1:T(8,128)}, f32[128,64]{0,1:T(8,128)S(1)}, u32[]{:S(2)}) copy-start(f32[128,64]{0,1:T(8,128)S(1)} %fusion.99) | copy-start | bytes 98308
  62.8 1.1 copy-start.1
  64.6 1.5 copy-start.4
  64.6 1.5 copy-start.5
  64.8 17.6 %collective-permute-start.3 = (f32[2,2,4,32,256]{4,3,2,1,0:T(8,128)S(1)}, f32[2,2,4,32,256]{4,3,2,1,0:T(8,128)S(1)}, u32[]{:S(2)}, u32[]{:S(2)}) collective-permute-start(f32[2,2,4,32,256]{4,3,2,1,0:T(8,128)S(1)} %get-tuple-element.38), channel_id=1, source_target_pairs={{2,0},{4,2},{6,4},{8,6},{10,8},{12,10},{14,12},{16,14},{18,16},{20... | collective-permute-start | bytes 1572872 | tf_op jit(solution)/shard_map/ppermute | solution.py:25
  66.2 27.2 %collective-permute-start.2 = (f32[2,2,4,32,256]{4,3,2,1,0:T(8,128)S(1)}, f32[2,2,4,32,256]{4,3,2,1,0:T(8,128)S(1)}, u32[]{:S(2)}, u32[]{:S(2)}) collective-permute-start(f32[2,2,4,32,256]{4,3,2,1,0:T(8,128)S(1)} %get-tuple-element.37), channel_id=1, source_target_pairs={{0,2},{2,4},{4,6},{6,8},{8,10},{10,12},{12,14},{14,16},{16,18},{18... | collective-permute-start | bytes 1572872 | tf_op jit(solution)/shard_map/ppermute | solution.py:23
  95.5 1.8 copy-start.3
  95.6 1.8 copy-start.7
  95.6 1.8 copy-start.8
  96.0 4.5 %collective-permute-start.5 = (f32[2,4,4,128]{3,2,1,0:T(4,128)S(1)}, f32[2,4,4,128]{3,2,1,0:T(4,128)S(1)}, u32[]{:S(2)}, u32[]{:S(2)}) collective-permute-start(f32[2,4,4,128]{3,2,1,0:T(4,128)S(1)} %get-tuple-element.47), channel_id=1, source_target_pairs={{1,0},{3,2},{5,4},{7,6},{9,8},{11,10},{13,12},{15,14},{17,16},{19,... | collective-permute-start | bytes 49160 | tf_op jit(solution)/shard_map/ppermute | solution.py:25
  97.4 3.9 %collective-permute-start.4 = (f32[2,4,4,128]{3,2,1,0:T(4,128)S(1)}, f32[2,4,4,128]{3,2,1,0:T(4,128)S(1)}, u32[]{:S(2)}, u32[]{:S(2)}) collective-permute-start(f32[2,4,4,128]{3,2,1,0:T(4,128)S(1)} %get-tuple-element.46), channel_id=1, source_target_pairs={{0,1},{2,3},{4,5},{6,7},{8,9},{10,11},{12,13},{14,15},{16,17},{18,... | collective-permute-start | bytes 49160 | tf_op jit(solution)/shard_map/ppermute | solution.py:23
  101.8 8.4 %collective-permute-start.6 = (f32[2,2,4,16,128]{4,3,2,1,0:T(8,128)S(1)}, f32[2,2,4,16,128]{4,3,2,1,0:T(8,128)S(1)}, u32[]{:S(2)}, u32[]{:S(2)}) collective-permute-start(f32[2,2,4,16,128]{4,3,2,1,0:T(8,128)S(1)} %pad_maximum_fusion.9), channel_id=1, source_target_pairs={{2,0},{4,2},{6,4},{8,6},{10,8},{12,10},{14,12},{16,14},{18,16},{20... | collective-permute-start | bytes 393224 | tf_op jit(solution)/shard_map/ppermute | solution.py:25
  103.1 9.1 %collective-permute-start.7 = (f32[2,2,4,16,128]{4,3,2,1,0:T(8,128)S(1)}, f32[2,2,4,16,128]{4,3,2,1,0:T(8,128)S(1)}, u32[]{:S(2)}, u32[]{:S(2)}) collective-permute-start(f32[2,2,4,16,128]{4,3,2,1,0:T(8,128)S(1)} %pad_maximum_fusion.9), channel_id=1, source_target_pairs={{0,2},{2,4},{4,6},{6,8},{8,10},{10,12},{12,14},{14,16},{16,18},{18... | collective-permute-start | bytes 393224 | tf_op jit(solution)/shard_map/ppermute | solution.py:23
  113.0 4.5 %collective-permute-start.9 = (f32[2,2,4,64]{3,2,1,0:T(4,128)S(1)}, f32[2,2,4,64]{3,2,1,0:T(4,128)S(1)}, u32[]{:S(2)}, u32[]{:S(2)}) collective-permute-start(f32[2,2,4,64]{3,2,1,0:T(4,128)S(1)} %get-tuple-element.51), channel_id=1, source_target_pairs={{1,0},{3,2},{5,4},{7,6},{9,8},{11,10},{13,12},{15,14},{17,16},{19,... | collective-permute-start | bytes 12296 | tf_op jit(solution)/shard_map/ppermute | solution.py:25
  114.4 3.8 %collective-permute-start.8 = (f32[2,2,4,64]{3,2,1,0:T(4,128)S(1)}, f32[2,2,4,64]{3,2,1,0:T(4,128)S(1)}, u32[]{:S(2)}, u32[]{:S(2)}) collective-permute-start(f32[2,2,4,64]{3,2,1,0:T(4,128)S(1)} %get-tuple-element.50), channel_id=1, source_target_pairs={{0,1},{2,3},{4,5},{6,7},{8,9},{10,11},{12,13},{14,15},{16,17},{18,... | collective-permute-start | bytes 12296 | tf_op jit(solution)/shard_map/ppermute | solution.py:23
  118.7 6.1 %collective-permute-start.10 = (f32[2,2,1,8,64]{4,3,1,0,2:T(8,128)S(1)}, f32[2,2,1,8,64]{4,3,1,0,2:T(8,128)S(1)}, u32[]{:S(2)}, u32[]{:S(2)}) collective-permute-start(f32[2,2,1,8,64]{4,3,1,0,2:T(8,128)S(1)} %maximum_bitcast_fusion.8), channel_id=1, source_target_pairs={{2,0},{4,2},{6,4},{8,6},{10,8},{12,10},{14,12},{16,14},{18,16},{20... | collective-permute-start | bytes 24584 | tf_op jit(solution)/shard_map/ppermute | solution.py:35
  124.7 6.3 %collective-permute-start.11 = (f32[2,2,1,8,64]{4,3,1,0,2:T(8,128)S(1)}, f32[2,2,1,8,64]{4,3,1,0,2:T(8,128)S(1)}, u32[]{:S(2)}, u32[]{:S(2)}) collective-permute-start(f32[2,2,1,8,64]{4,3,1,0,2:T(8,128)S(1)} %bitcast.179), channel_id=1, source_target_pairs={{0,2},{2,4},{4,6},{6,8},{8,10},{10,12},{12,14},{14,16},{16,18},{18... | collective-permute-start | bytes 24584 | tf_op jit(solution)/shard_map/ppermute | solution.py:35
  131.0 5.9 %collective-permute-start.12 = (f32[2,2,1,8,64]{4,3,1,0,2:T(8,128)S(1)}, f32[2,2,1,8,64]{4,3,1,0,2:T(8,128)S(1)}, u32[]{:S(2)}, u32[]{:S(2)}) collective-permute-start(f32[2,2,1,8,64]{4,3,1,0,2:T(8,128)S(1)} %fusion.123), channel_id=1, source_target_pairs={{2,0},{4,2},{6,4},{8,6},{10,8},{12,10},{14,12},{16,14},{18,16},{20... | collective-permute-start | bytes 24584 | tf_op jit(solution)/shard_map/ppermute | solution.py:35
  136.9 6.3 %collective-permute-start.13 = (f32[2,2,1,8,64]{4,3,1,0,2:T(8,128)S(1)}, f32[2,2,1,8,64]{4,3,1,0,2:T(8,128)S(1)}, u32[]{:S(2)}, u32[]{:S(2)}) collective-permute-start(f32[2,2,1,8,64]{4,3,1,0,2:T(8,128)S(1)} %bitcast.189), channel_id=1, source_target_pairs={{0,2},{2,4},{4,6},{6,8},{8,10},{10,12},{12,14},{14,16},{16,18},{18... | collective-permute-start | bytes 24584 | tf_op jit(solution)/shard_map/ppermute | solution.py:35
  181.6 3.1 %collective-permute-start.14 = (f32[2,16,1,32]{3,1,2,0:T(8,128)S(1)}, f32[2,16,1,32]{3,1,2,0:T(8,128)S(1)}, u32[]{:S(2)}, u32[]{:S(2)}) collective-permute-start(f32[2,16,1,32]{3,1,2,0:T(8,128)S(1)} %slice.751), channel_id=1, source_target_pairs={{1,0},{3,2},{5,4},{7,6},{9,8},{11,10},{13,12},{15,14},{17,16},{19,... | collective-permute-start | bytes 12296 | tf_op jit(solution)/shard_map/ppermute | solution.py:35
  184.8 2.9 %collective-permute-start.15 = (f32[2,16,1,32]{3,1,2,0:T(8,128)S(1)}, f32[2,16,1,32]{3,1,2,0:T(8,128)S(1)}, u32[]{:S(2)}, u32[]{:S(2)}) collective-permute-start(f32[2,16,1,32]{3,1,2,0:T(8,128)S(1)} %slice.753), channel_id=1, source_target_pairs={{0,1},{2,3},{4,5},{6,7},{8,9},{10,11},{12,13},{14,15},{16,17},{18,... | collective-permute-start | bytes 12296 | tf_op jit(solution)/shard_map/ppermute | solution.py:35
  187.7 3.1 %collective-permute-start.16 = (f32[2,16,1,32]{3,1,2,0:T(8,128)S(1)}, f32[2,16,1,32]{3,1,2,0:T(8,128)S(1)}, u32[]{:S(2)}, u32[]{:S(2)}) collective-permute-start(f32[2,16,1,32]{3,1,2,0:T(8,128)S(1)} %slice.757), channel_id=1, source_target_pairs={{1,0},{3,2},{5,4},{7,6},{9,8},{11,10},{13,12},{15,14},{17,16},{19,... | collective-permute-start | bytes 12296 | tf_op jit(solution)/shard_map/ppermute | solution.py:35
  190.8 4.3 %collective-permute-start.17 = (f32[2,16,1,32]{3,1,2,0:T(8,128)S(1)}, f32[2,16,1,32]{3,1,2,0:T(8,128)S(1)}, u32[]{:S(2)}, u32[]{:S(2)}) collective-permute-start(f32[2,16,1,32]{3,1,2,0:T(8,128)S(1)} %slice.759), channel_id=1, source_target_pairs={{0,1},{2,3},{4,5},{6,7},{8,9},{10,11},{12,13},{14,15},{16,17},{18,... | collective-permute-start | bytes 12296 | tf_op jit(solution)/shard_map/ppermute | solution.py:35
where the time goes:
time: 197 us; the launch traced here: 196 us
  local copies, waits for them, and re-layouts  59.7 us (30%)
  starting transfers between devices  45.2 us (23%)
  waiting for transfers between devices  43.5 us (22%)
  blocking collectives  38.1 us (19%)
  other arithmetic  5.06 us (3%)
  matrix products  2.78 us (1%)
  between operations  2.1 us (1%)
    all_gather x1, blocking collectives, per_device(): whole = lax.all_gather(volume, 'wide', axis=0, tiled=True)  38.1 us
    slice x8, local copies, waits for them, and re-layouts, lift_general(): odd_part = lax.slice_in_dim(volume, 1, length, 2, along)  26.5 us
    slice x11, local copies, waits for them, and re-layouts, lift_general(): even_part = lax.slice_in_dim(volume, 0, length, 2, along)  25.1 us
    ppermute x5, starting transfers between devices, extended(): lax.ppermute(tail, axis, [(i, (i + 1) % count) for i in range(ends)])  19.8 us
    ppermute x8, starting transfers between devices, shifted(): lax.ppermute(value, axis, [(source, source + steps) for source in range(f...  18.9 us
    ppermute x8, waiting for transfers between devices, shifted(): lax.ppermute(value, axis, [(source, source + steps) for source in range(f...  16.5 us
    ppermute x5, waiting for transfers between devices, extended(): lax.ppermute(tail, axis, [(i, (i + 1) % count) for i in range(ends)])  14.6 us
    ppermute x5, waiting for transfers between devices, extended(): lax.ppermute(head, axis, [((i + 1) % count, i) for i in range(ends)])  12.5 us
  transfers between devices with their start and end apart: 18, of which 13 were waited for; matrix products, arithmetic and copies ran while one was open for 8% of the time, Pallas kernels for 0%

commit v1 on v0

--- a/solution.py
+++ b/solution.py
@@ -10,6 +10,12 @@
 LIFT_DELTA = 0.4435068522
 LIFT_ZETA = 1.149604398
 LIFT_INVERSE = 1.0 / 1.149604398
+
+
+def laid_out(blocks, dim):
+    blocks = jnp.moveaxis(blocks, 0, dim)
+    shape = blocks.shape
+    return blocks.reshape(*shape[:dim], shape[dim] * shape[dim + 1], *shape[dim + 2 :])
 
 
 def extended(cells, sides, width):
@@ -135,7 +141,19 @@
         band_set = z_pair.reshape((8,) + z_pair.shape[3:])
         details.append(band_set[1:])
         volume = band_set[0]
-    whole = lax.all_gather(volume, "wide", axis=0, tiled=True)
+    length_2 = lax.axis_size("wide")
+    pairs = [(i_2, (i_2 + 1) % length_2) for i_2 in range(length_2)]
+    back = [(b, a) for a, b in pairs]
+    lower, upper = ([], [])
+    for step in range(length_2 - 1):
+        if step % 2 == 0:
+            lower.append(lax.ppermute(lower[-1] if lower else volume, "wide", pairs))
+        else:
+            upper.append(lax.ppermute(upper[-1] if upper else volume, "wide", back))
+    tiles = jnp.stack([*lower[::-1], volume, *upper])
+    shift = lax.axis_index("wide") - len(lower)
+    tiles = tiles[(jnp.arange(length_2) - shift) % length_2]
+    whole = laid_out(tiles, 0)
     x_pair = lift_columns(whole)
     y_pair = lift_general(x_pair, 2, pull_next_y, pull_prev_y, narrow_first, narrow_last)
     z_pair = lift_local(y_pair, 2)

time: 197 us -> 217 us (1.10)
  starting transfers between devices: 45.2 us -> 87.4 us
  blocking collectives: 38.1 us -> 0 us
  waiting for transfers between devices: 43.5 us -> 58.8 us
    ppermute x0 -> x15, starting transfers between devices: none -> 42.2 us  [the longest x7 39.9 us: per_device(): upper.append(lax.ppermute(upper[-1] if upper else volume, 'wide', back))]
    all_gather x1 -> x0, blocking collectives: 38.1 us -> none  [per_device(): whole = lax.all_gather(volume, 'wide', axis=0, tiled=True)]
    ppermute x0 -> x15, waiting for transfers between devices: none -> 15.2 us  [the longest x8 15.2 us: per_device(): lower.append(lax.ppermute(lower[-1] if lower else volume, 'wide', pairs))]
  transfers between devices with their start and end apart: 18 -> 33, of which waited for: 13 -> 21; matrix products, arithmetic and copies ran while one was open for 8% -> 7% of each run, Pallas kernels for 0% -> 0%
where the time goes in v1:
time: 217 us
  starting transfers between devices  87.4 us (40%)
  local copies, waits for them, and re-layouts  60.3 us (28%)
  waiting for transfers between devices  58.8 us (27%)
  other arithmetic  5.07 us (2%)
  matrix products  2.78 us (1%)
  between operations  2.27 us (1%)
    ppermute x7, starting transfers between devices, per_device(): upper.append(lax.ppermute(upper[-1] if upper else volume, 'wide', back))  39.9 us
    slice x8, local copies, waits for them, and re-layouts, lift_general(): odd_part = lax.slice_in_dim(volume, 1, length, 2, along)  26.5 us
    slice x11, local copies, waits for them, and re-layouts, lift_general(): even_part = lax.slice_in_dim(volume, 0, length, 2, along)  25.1 us
    ppermute x5, starting transfers between devices, extended(): lax.ppermute(tail, axis, [(i, (i + 1) % count) for i in range(ends)])  19.8 us
    ppermute x8, starting transfers between devices, shifted(): lax.ppermute(value, axis, [(source, source + steps) for source in range(f...  18.9 us
    ppermute x8, waiting for transfers between devices, shifted(): lax.ppermute(value, axis, [(source, source + steps) for source in range(f...  16.6 us
    ppermute x8, waiting for transfers between devices, per_device(): lower.append(lax.ppermute(lower[-1] if lower else volume, 'wide', pairs))  15.2 us
    ppermute x5, waiting for transfers between devices, extended(): lax.ppermute(tail, axis, [(i, (i + 1) % count) for i in range(ends)])  14.6 us
  transfers between devices with their start and end apart: 33, of which 21 were waited for; matrix products, arithmetic and copies ran while one was open for 7% of the time, Pallas kernels for 0%

profile of v1, /device:TPU:0, one launch (start us, length us, event | category | flops | bytes accessed | tf_op | source)
XLA Modules:
  0.0 216.7 jit_solution(10351238507695750786)
XLA Ops:
  0.8 19.5 %slice.508 = f32[512,256]{1,0:T(8,128)S(1)} slice(f32[512,512]{1,0:T(8,128)S(1)} %fusion.14), slice={[0:512:1], [1:512:2]} | slice | bytes 1048576 | tf_op jit(solution)/shard_map/slice | solution.py:52
  20.2 19.5 %slice.507 = f32[512,256]{1,0:T(8,128)S(1)} slice(f32[512,512]{1,0:T(8,128)S(1)} %fusion.14), slice={[0:512:1], [0:512:2]} | slice | bytes 1048576 | tf_op jit(solution)/shard_map/slice | solution.py:51
  41.2 1.9 convolution_bitcast_fusion
  43.1 1.3 collective-permute-start.1
  44.4 3.2 %collective-permute-start = (f32[2,8,4,256]{3,2,1,0:T(4,128)S(1)}, f32[2,8,4,256]{3,2,1,0:T(4,128)S(1)}, u32[]{:S(2)}, u32[]{:S(2)}) collective-permute-start(f32[2,8,4,256]{3,2,1,0:T(4,128)S(1)} %get-tuple-element.40), channel_id=1, source_target_pairs={{0,1},{2,3},{4,5},{6,7},{8,9},{10,11},{12,13},{14,15},{16,17},{18,... | collective-permute-start | bytes 196616 | tf_op jit(solution)/shard_map/ppermute | solution.py:29
  47.7 4.5 %slice.549 = f32[256,128]{1,0:T(8,128)S(1)} slice(f32[256,256]{1,0:T(8,128)S(1)} %fusion.40), slice={[0:256:1], [1:256:2]} | slice | bytes 262144 | tf_op jit(solution)/shard_map/slice | solution.py:52
  52.2 4.5 %slice.548 = f32[256,128]{1,0:T(8,128)S(1)} slice(f32[256,256]{1,0:T(8,128)S(1)} %fusion.40), slice={[0:256:1], [0:256:2]} | slice | bytes 262144 | tf_op jit(solution)/shard_map/slice | solution.py:51
  60.6 2.2 %slice.522 = f32[2,8,36,256]{3,2,1,0:T(8,128)} slice(f32[2,8,72,256]{3,2,1,0:T(8,128)S(1)} %pad_maximum_fusion.1), slice={[0:2:1], [0:8:1], [1:72:2], [0:256:1]} | slice | bytes 1179648 | tf_op jit(solution)/shard_map/slice | solution.py:52
  64.8 1.3 collective-permute-start.3
  66.2 5.5 %collective-permute-start.2 = (f32[2,2,4,32,256]{4,3,2,1,0:T(8,128)S(1)}, f32[2,2,4,32,256]{4,3,2,1,0:T(8,128)S(1)}, u32[]{:S(2)}, u32[]{:S(2)}) collective-permute-start(f32[2,2,4,32,256]{4,3,2,1,0:T(8,128)S(1)} %get-tuple-element.37), channel_id=1, source_target_pairs={{0,2},{2,4},{4,6},{6,8},{8,10},{10,12},{12,14},{14,16},{16,18},{18... | collective-permute-start | bytes 1572872 | tf_op jit(solution)/shard_map/ppermute | solution.py:29
  72.0 10.4 %collective-permute-done.3 = f32[2,2,4,32,256]{4,3,2,1,0:T(8,128)S(1)} collective-permute-done((f32[2,2,4,32,256]{4,3,2,1,0:T(8,128)S(1)}, f32[2,2,4,32,256]{4,3,2,1,0:T(8,128)S(1)}, u32[]{:S(2)}, u32[]{:S(2)}) %collective-permute-start.3) | collective-permute-done | bytes 524320 | tf_op jit(solution)/shard_map/ppermute | solution.py:31
  82.5 11.0 %collective-permute-done.2 = f32[2,2,4,32,256]{4,3,2,1,0:T(8,128)S(1)} collective-permute-done((f32[2,2,4,32,256]{4,3,2,1,0:T(8,128)S(1)}, f32[2,2,4,32,256]{4,3,2,1,0:T(8,128)S(1)}, u32[]{:S(2)}, u32[]{:S(2)}) %collective-permute-start.2) | collective-permute-done | bytes 524320 | tf_op jit(solution)/shard_map/ppermute | solution.py:29
  96.0 1.3 collective-permute-start.5
  97.5 3.0 %collective-permute-start.4 = (f32[2,4,4,128]{3,2,1,0:T(4,128)S(1)}, f32[2,4,4,128]{3,2,1,0:T(4,128)S(1)}, u32[]{:S(2)}, u32[]{:S(2)}) collective-permute-start(f32[2,4,4,128]{3,2,1,0:T(4,128)S(1)} %get-tuple-element.46), channel_id=1, source_target_pairs={{0,1},{2,3},{4,5},{6,7},{8,9},{10,11},{12,13},{14,15},{16,17},{18,... | collective-permute-start | bytes 49160 | tf_op jit(solution)/shard_map/ppermute | solution.py:29
  101.8 1.3 collective-permute-start.6
  103.1 5.0 %collective-permute-start.7 = (f32[2,2,4,16,128]{4,3,2,1,0:T(8,128)S(1)}, f32[2,2,4,16,128]{4,3,2,1,0:T(8,128)S(1)}, u32[]{:S(2)}, u32[]{:S(2)}) collective-permute-start(f32[2,2,4,16,128]{4,3,2,1,0:T(8,128)S(1)} %pad_maximum_fusion.9), channel_id=1, source_target_pairs={{0,2},{2,4},{4,6},{6,8},{8,10},{10,12},{12,14},{14,16},{16,18},{18... | collective-permute-start | bytes 393224 | tf_op jit(solution)/shard_map/ppermute | solution.py:29
  108.2 2.0 collective-permute-done.6
  110.2 2.0 collective-permute-done.7
  113.0 1.3 collective-permute-start.9
  114.4 3.0 %collective-permute-start.8 = (f32[2,2,4,64]{3,2,1,0:T(4,128)S(1)}, f32[2,2,4,64]{3,2,1,0:T(4,128)S(1)}, u32[]{:S(2)}, u32[]{:S(2)}) collective-permute-start(f32[2,2,4,64]{3,2,1,0:T(4,128)S(1)} %get-tuple-element.50), channel_id=1, source_target_pairs={{0,1},{2,3},{4,5},{6,7},{8,9},{10,11},{12,13},{14,15},{16,17},{18,... | collective-permute-start | bytes 12296 | tf_op jit(solution)/shard_map/ppermute | solution.py:29
  118.6 1.3 collective-permute-start.10
  119.9 4.8 %collective-permute-done.10 = f32[2,2,1,8,64]{4,3,1,0,2:T(8,128)S(1)} collective-permute-done((f32[2,2,1,8,64]{4,3,1,0,2:T(8,128)S(1)}, f32[2,2,1,8,64]{4,3,1,0,2:T(8,128)S(1)}, u32[]{:S(2)}, u32[]{:S(2)}) %collective-permute-start.10) | collective-permute-done | bytes 8224 | tf_op jit(solution)/shard_map/ppermute | solution.py:41
  124.7 4.8 %collective-permute-start.11 = (f32[2,2,1,8,64]{4,3,1,0,2:T(8,128)S(1)}, f32[2,2,1,8,64]{4,3,1,0,2:T(8,128)S(1)}, u32[]{:S(2)}, u32[]{:S(2)}) collective-permute-start(f32[2,2,1,8,64]{4,3,1,0,2:T(8,128)S(1)} %bitcast.246), channel_id=1, source_target_pairs={{0,2},{2,4},{4,6},{6,8},{8,10},{10,12},{12,14},{14,16},{16,18},{18... | collective-permute-start | bytes 24584 | tf_op jit(solution)/shard_map/ppermute | solution.py:41
  129.5 1.4 collective-permute-done.11
  132.2 4.6 %collective-permute-done.12 = f32[2,2,1,8,64]{4,3,1,0,2:T(8,128)S(1)} collective-permute-done((f32[2,2,1,8,64]{4,3,1,0,2:T(8,128)S(1)}, f32[2,2,1,8,64]{4,3,1,0,2:T(8,128)S(1)}, u32[]{:S(2)}, u32[]{:S(2)}) %collective-permute-start.12) | collective-permute-done | bytes 8224 | tf_op jit(solution)/shard_map/ppermute | solution.py:41
  136.9 4.8 %collective-permute-start.13 = (f32[2,2,1,8,64]{4,3,1,0,2:T(8,128)S(1)}, f32[2,2,1,8,64]{4,3,1,0,2:T(8,128)S(1)}, u32[]{:S(2)}, u32[]{:S(2)}) collective-permute-start(f32[2,2,1,8,64]{4,3,1,0,2:T(8,128)S(1)} %bitcast.255), channel_id=1, source_target_pairs={{0,2},{2,4},{4,6},{6,8},{8,10},{10,12},{12,14},{14,16},{16,18},{18... | collective-permute-start | bytes 24584 | tf_op jit(solution)/shard_map/ppermute | solution.py:41
  141.7 1.4 collective-permute-done.13
  143.2 2.4 %collective-permute-start.14 = (f32[1,8,64]{2,1,0:T(8,128)S(1)}, f32[1,8,64]{2,1,0:T(8,128)S(1)}, u32[]{:S(2)}, u32[]{:S(2)}) collective-permute-start(f32[1,8,64]{2,1,0:T(8,128)S(1)} %slice_bitcast_fusion.4), channel_id=1, source_target_pairs={{0,2},{2,4},{4,6},{6,8},{8,10},{10,12},{12,14},{14,16},{16,18},{18... | collective-permute-start | bytes 6152 | tf_op jit(solution)/shard_map/ppermute | solution.py:150
  145.5 4.9 %collective-permute-done.14 = f32[1,8,64]{2,1,0:T(8,128)S(1)} collective-permute-done((f32[1,8,64]{2,1,0:T(8,128)S(1)}, f32[1,8,64]{2,1,0:T(8,128)S(1)}, u32[]{:S(2)}, u32[]{:S(2)}) %collective-permute-start.14) | collective-permute-done | bytes 2080 | tf_op jit(solution)/shard_map/ppermute | solution.py:150
  150.5 5.7 %collective-permute-start.22 = (f32[1,8,64]{2,1,0:T(8,128)S(1)}, f32[1,8,64]{2,1,0:T(8,128)S(1)}, u32[]{:S(2)}, u32[]{:S(2)}) collective-permute-start(f32[1,8,64]{2,1,0:T(8,128)S(1)} %slice_bitcast_fusion.4), channel_id=1, source_target_pairs={{2,0},{4,2},{6,4},{8,6},{10,8},{12,10},{14,12},{16,14},{18,16},{20... | collective-permute-start | bytes 6152 | tf_op jit(solution)/shard_map/ppermute | solution.py:152
  156.1 1.5 collective-permute-done.15
  157.7 5.7 %collective-permute-start.23 = (f32[1,8,64]{2,1,0:T(8,128)S(1)}, f32[1,8,64]{2,1,0:T(8,128)S(1)}, u32[]{:S(2)}, u32[]{:S(2)}) collective-permute-start(f32[1,8,64]{2,1,0:T(8,128)S(1)} %collective-permute-done.22), channel_id=1, source_target_pairs={{2,0},{4,2},{6,4},{8,6},{10,8},{12,10},{14,12},{16,14},{18,16},{20... | collective-permute-start | bytes 6152 | tf_op jit(solution)/shard_map/ppermute | solution.py:152
  163.3 1.5 collective-permute-done.16
  164.9 5.7 %collective-permute-start.24 = (f32[1,8,64]{2,1,0:T(8,128)S(1)}, f32[1,8,64]{2,1,0:T(8,128)S(1)}, u32[]{:S(2)}, u32[]{:S(2)}) collective-permute-start(f32[1,8,64]{2,1,0:T(8,128)S(1)} %collective-permute-done.23), channel_id=1, source_target_pairs={{2,0},{4,2},{6,4},{8,6},{10,8},{12,10},{14,12},{16,14},{18,16},{20... | collective-permute-start | bytes 6152 | tf_op jit(solution)/shard_map/ppermute | solution.py:152
  170.6 1.5 collective-permute-done.17
  172.1 5.7 %collective-permute-start.25 = (f32[1,8,64]{2,1,0:T(8,128)S(1)}, f32[1,8,64]{2,1,0:T(8,128)S(1)}, u32[]{:S(2)}, u32[]{:S(2)}) collective-permute-start(f32[1,8,64]{2,1,0:T(8,128)S(1)} %collective-permute-done.24), channel_id=1, source_target_pairs={{2,0},{4,2},{6,4},{8,6},{10,8},{12,10},{14,12},{16,14},{18,16},{20... | collective-permute-start | bytes 6152 | tf_op jit(solution)/shard_map/ppermute | solution.py:152
  177.8 1.5 collective-permute-done.18
  179.3 5.7 %collective-permute-start.26 = (f32[1,8,64]{2,1,0:T(8,128)S(1)}, f32[1,8,64]{2,1,0:T(8,128)S(1)}, u32[]{:S(2)}, u32[]{:S(2)}) collective-permute-start(f32[1,8,64]{2,1,0:T(8,128)S(1)} %collective-permute-done.25), channel_id=1, source_target_pairs={{2,0},{4,2},{6,4},{8,6},{10,8},{12,10},{14,12},{16,14},{18,16},{20... | collective-permute-start | bytes 6152 | tf_op jit(solution)/shard_map/ppermute | solution.py:152
  185.0 1.5 collective-permute-done.19
  186.5 5.7 %collective-permute-start.27 = (f32[1,8,64]{2,1,0:T(8,128)S(1)}, f32[1,8,64]{2,1,0:T(8,128)S(1)}, u32[]{:S(2)}, u32[]{:S(2)}) collective-permute-start(f32[1,8,64]{2,1,0:T(8,128)S(1)} %collective-permute-done.26), channel_id=1, source_target_pairs={{2,0},{4,2},{6,4},{8,6},{10,8},{12,10},{14,12},{16,14},{18,16},{20... | collective-permute-start | bytes 6152 | tf_op jit(solution)/shard_map/ppermute | solution.py:152
  192.2 1.5 collective-permute-done.20
  193.7 5.7 %collective-permute-start.28 = (f32[1,8,64]{2,1,0:T(8,128)S(1)}, f32[1,8,64]{2,1,0:T(8,128)S(1)}, u32[]{:S(2)}, u32[]{:S(2)}) collective-permute-start(f32[1,8,64]{2,1,0:T(8,128)S(1)} %collective-permute-done.27), channel_id=1, source_target_pairs={{2,0},{4,2},{6,4},{8,6},{10,8},{12,10},{14,12},{16,14},{18,16},{20... | collective-permute-start | bytes 6152 | tf_op jit(solution)/shard_map/ppermute | solution.py:152
  199.4 1.5 collective-permute-done.21
  201.9 1.3 collective-permute-start.29
  203.2 1.8 collective-permute-done.29
  205.0 2.1 collective-permute-start.30
  209.3 1.8 collective-permute-done.31
  211.1 2.1 collective-permute-start.32
  (243 shorter events, 21.3 us)
Async XLA Ops:
  0.6 40.6 %copy-start = (f32[8,64,512]{2,1,0:T(8,128)S(1)}, f32[8,64,512]{2,1,0:T(8,128)}, u32[]{:S(2)}) copy-start(f32[8,64,512]{2,1,0:T(8,128)} %param.1) | copy-start | bytes 3145732
  43.1 16.6 %collective-permute-start.1 = (f32[2,8,4,256]{3,2,1,0:T(4,128)S(1)}, f32[2,8,4,256]{3,2,1,0:T(4,128)S(1)}, u32[]{:S(2)}, u32[]{:S(2)}) collective-permute-start(f32[2,8,4,256]{3,2,1,0:T(4,128)S(1)} %get-tuple-element.41), channel_id=1, source_target_pairs={{1,0},{3,2},{5,4},{7,6},{9,8},{11,10},{13,12},{15,14},{17,16},{19,... | collective-permute-start | bytes 196616 | tf_op jit(solution)/shard_map/ppermute | solution.py:31
  44.4 15.3 %collective-permute-start = (f32[2,8,4,256]{3,2,1,0:T(4,128)S(1)}, f32[2,8,4,256]{3,2,1,0:T(4,128)S(1)}, u32[]{:S(2)}, u32[]{:S(2)}) collective-permute-start(f32[2,8,4,256]{3,2,1,0:T(4,128)S(1)} %get-tuple-element.40), channel_id=1, source_target_pairs={{0,1},{2,3},{4,5},{6,7},{8,9},{10,11},{12,13},{14,15},{16,17},{18,... | collective-permute-start | bytes 196616 | tf_op jit(solution)/shard_map/ppermute | solution.py:29
  57.0 2.8 %copy-start.6 = (f32[128,64]{0,1:T(8,128)}, f32[128,64]{0,1:T(8,128)S(1)}, u32[]{:S(2)}) copy-start(f32[128,64]{0,1:T(8,128)S(1)} %fusion.97) | copy-start | bytes 98308
  57.3 2.5 %copy-start.2 = (f32[128,64]{0,1:T(8,128)}, f32[128,64]{0,1:T(8,128)S(1)}, u32[]{:S(2)}) copy-start(f32[128,64]{0,1:T(8,128)S(1)} %fusion.99) | copy-start | bytes 98308
  62.8 1.1 copy-start.1
  64.6 1.5 copy-start.4
  64.6 1.5 copy-start.5
  64.8 17.6 %collective-permute-start.3 = (f32[2,2,4,32,256]{4,3,2,1,0:T(8,128)S(1)}, f32[2,2,4,32,256]{4,3,2,1,0:T(8,128)S(1)}, u32[]{:S(2)}, u32[]{:S(2)}) collective-permute-start(f32[2,2,4,32,256]{4,3,2,1,0:T(8,128)S(1)} %get-tuple-element.38), channel_id=1, source_target_pairs={{2,0},{4,2},{6,4},{8,6},{10,8},{12,10},{14,12},{16,14},{18,16},{20... | collective-permute-start | bytes 1572872 | tf_op jit(solution)/shard_map/ppermute | solution.py:31
  66.2 27.2 %collective-permute-start.2 = (f32[2,2,4,32,256]{4,3,2,1,0:T(8,128)S(1)}, f32[2,2,4,32,256]{4,3,2,1,0:T(8,128)S(1)}, u32[]{:S(2)}, u32[]{:S(2)}) collective-permute-start(f32[2,2,4,32,256]{4,3,2,1,0:T(8,128)S(1)} %get-tuple-element.37), channel_id=1, source_target_pairs={{0,2},{2,4},{4,6},{6,8},{8,10},{10,12},{12,14},{14,16},{16,18},{18... | collective-permute-start | bytes 1572872 | tf_op jit(solution)/shard_map/ppermute | solution.py:29
  95.6 1.8 copy-start.3
  95.6 1.8 copy-start.7
  95.6 1.8 copy-start.8
  96.0 4.5 %collective-permute-start.5 = (f32[2,4,4,128]{3,2,1,0:T(4,128)S(1)}, f32[2,4,4,128]{3,2,1,0:T(4,128)S(1)}, u32[]{:S(2)}, u32[]{:S(2)}) collective-permute-start(f32[2,4,4,128]{3,2,1,0:T(4,128)S(1)} %get-tuple-element.47), channel_id=1, source_target_pairs={{1,0},{3,2},{5,4},{7,6},{9,8},{11,10},{13,12},{15,14},{17,16},{19,... | collective-permute-start | bytes 49160 | tf_op jit(solution)/shard_map/ppermute | solution.py:31
  97.5 3.9 %collective-permute-start.4 = (f32[2,4,4,128]{3,2,1,0:T(4,128)S(1)}, f32[2,4,4,128]{3,2,1,0:T(4,128)S(1)}, u32[]{:S(2)}, u32[]{:S(2)}) collective-permute-start(f32[2,4,4,128]{3,2,1,0:T(4,128)S(1)} %get-tuple-element.46), channel_id=1, source_target_pairs={{0,1},{2,3},{4,5},{6,7},{8,9},{10,11},{12,13},{14,15},{16,17},{18,... | collective-permute-start | bytes 49160 | tf_op jit(solution)/shard_map/ppermute | solution.py:29
  101.8 8.4 %collective-permute-start.6 = (f32[2,2,4,16,128]{4,3,2,1,0:T(8,128)S(1)}, f32[2,2,4,16,128]{4,3,2,1,0:T(8,128)S(1)}, u32[]{:S(2)}, u32[]{:S(2)}) collective-permute-start(f32[2,2,4,16,128]{4,3,2,1,0:T(8,128)S(1)} %pad_maximum_fusion.9), channel_id=1, source_target_pairs={{2,0},{4,2},{6,4},{8,6},{10,8},{12,10},{14,12},{16,14},{18,16},{20... | collective-permute-start | bytes 393224 | tf_op jit(solution)/shard_map/ppermute | solution.py:31
  103.1 9.1 %collective-permute-start.7 = (f32[2,2,4,16,128]{4,3,2,1,0:T(8,128)S(1)}, f32[2,2,4,16,128]{4,3,2,1,0:T(8,128)S(1)}, u32[]{:S(2)}, u32[]{:S(2)}) collective-permute-start(f32[2,2,4,16,128]{4,3,2,1,0:T(8,128)S(1)} %pad_maximum_fusion.9), channel_id=1, source_target_pairs={{0,2},{2,4},{4,6},{6,8},{8,10},{10,12},{12,14},{14,16},{16,18},{18... | collective-permute-start | bytes 393224 | tf_op jit(solution)/shard_map/ppermute | solution.py:29
  113.0 4.4 %collective-permute-start.9 = (f32[2,2,4,64]{3,2,1,0:T(4,128)S(1)}, f32[2,2,4,64]{3,2,1,0:T(4,128)S(1)}, u32[]{:S(2)}, u32[]{:S(2)}) collective-permute-start(f32[2,2,4,64]{3,2,1,0:T(4,128)S(1)} %get-tuple-element.51), channel_id=1, source_target_pairs={{1,0},{3,2},{5,4},{7,6},{9,8},{11,10},{13,12},{15,14},{17,16},{19,... | collective-permute-start | bytes 12296 | tf_op jit(solution)/shard_map/ppermute | solution.py:31
  114.4 3.8 %collective-permute-start.8 = (f32[2,2,4,64]{3,2,1,0:T(4,128)S(1)}, f32[2,2,4,64]{3,2,1,0:T(4,128)S(1)}, u32[]{:S(2)}, u32[]{:S(2)}) collective-permute-start(f32[2,2,4,64]{3,2,1,0:T(4,128)S(1)} %get-tuple-element.50), channel_id=1, source_target_pairs={{0,1},{2,3},{4,5},{6,7},{8,9},{10,11},{12,13},{14,15},{16,17},{18,... | collective-permute-start | bytes 12296 | tf_op jit(solution)/shard_map/ppermute | solution.py:29
  118.6 6.1 %collective-permute-start.10 = (f32[2,2,1,8,64]{4,3,1,0,2:T(8,128)S(1)}, f32[2,2,1,8,64]{4,3,1,0,2:T(8,128)S(1)}, u32[]{:S(2)}, u32[]{:S(2)}) collective-permute-start(f32[2,2,1,8,64]{4,3,1,0,2:T(8,128)S(1)} %maximum_bitcast_fusion.8), channel_id=1, source_target_pairs={{2,0},{4,2},{6,4},{8,6},{10,8},{12,10},{14,12},{16,14},{18,16},{20... | collective-permute-start | bytes 24584 | tf_op jit(solution)/shard_map/ppermute | solution.py:41
  124.7 6.3 %collective-permute-start.11 = (f32[2,2,1,8,64]{4,3,1,0,2:T(8,128)S(1)}, f32[2,2,1,8,64]{4,3,1,0,2:T(8,128)S(1)}, u32[]{:S(2)}, u32[]{:S(2)}) collective-permute-start(f32[2,2,1,8,64]{4,3,1,0,2:T(8,128)S(1)} %bitcast.246), channel_id=1, source_target_pairs={{0,2},{2,4},{4,6},{6,8},{8,10},{10,12},{12,14},{14,16},{16,18},{18... | collective-permute-start | bytes 24584 | tf_op jit(solution)/shard_map/ppermute | solution.py:41
  131.0 5.9 %collective-permute-start.12 = (f32[2,2,1,8,64]{4,3,1,0,2:T(8,128)S(1)}, f32[2,2,1,8,64]{4,3,1,0,2:T(8,128)S(1)}, u32[]{:S(2)}, u32[]{:S(2)}) collective-permute-start(f32[2,2,1,8,64]{4,3,1,0,2:T(8,128)S(1)} %fusion.123), channel_id=1, source_target_pairs={{2,0},{4,2},{6,4},{8,6},{10,8},{12,10},{14,12},{16,14},{18,16},{20... | collective-permute-start | bytes 24584 | tf_op jit(solution)/shard_map/ppermute | solution.py:41
  136.9 6.3 %collective-permute-start.13 = (f32[2,2,1,8,64]{4,3,1,0,2:T(8,128)S(1)}, f32[2,2,1,8,64]{4,3,1,0,2:T(8,128)S(1)}, u32[]{:S(2)}, u32[]{:S(2)}) collective-permute-start(f32[2,2,1,8,64]{4,3,1,0,2:T(8,128)S(1)} %bitcast.255), channel_id=1, source_target_pairs={{0,2},{2,4},{4,6},{6,8},{8,10},{10,12},{12,14},{14,16},{16,18},{18... | collective-permute-start | bytes 24584 | tf_op jit(solution)/shard_map/ppermute | solution.py:41
  143.2 7.3 %collective-permute-start.14 = (f32[1,8,64]{2,1,0:T(8,128)S(1)}, f32[1,8,64]{2,1,0:T(8,128)S(1)}, u32[]{:S(2)}, u32[]{:S(2)}) collective-permute-start(f32[1,8,64]{2,1,0:T(8,128)S(1)} %slice_bitcast_fusion.4), channel_id=1, source_target_pairs={{0,2},{2,4},{4,6},{6,8},{8,10},{10,12},{12,14},{14,16},{16,18},{18... | collective-permute-start | bytes 6152 | tf_op jit(solution)/shard_map/ppermute | solution.py:150
  150.4 7.2 %collective-permute-start.15 = (f32[1,8,64]{2,1,0:T(8,128)S(1)}, f32[1,8,64]{2,1,0:T(8,128)S(1)}, u32[]{:S(2)}, u32[]{:S(2)}) collective-permute-start(f32[1,8,64]{2,1,0:T(8,128)S(1)} %collective-permute-done.14), channel_id=1, source_target_pairs={{0,2},{2,4},{4,6},{6,8},{8,10},{10,12},{12,14},{14,16},{16,18},{18... | collective-permute-start | bytes 6152 | tf_op jit(solution)/shard_map/ppermute | solution.py:150
  150.5 7.2 %collective-permute-start.22 = (f32[1,8,64]{2,1,0:T(8,128)S(1)}, f32[1,8,64]{2,1,0:T(8,128)S(1)}, u32[]{:S(2)}, u32[]{:S(2)}) collective-permute-start(f32[1,8,64]{2,1,0:T(8,128)S(1)} %slice_bitcast_fusion.4), channel_id=1, source_target_pairs={{2,0},{4,2},{6,4},{8,6},{10,8},{12,10},{14,12},{16,14},{18,16},{20... | collective-permute-start | bytes 6152 | tf_op jit(solution)/shard_map/ppermute | solution.py:152
  157.6 7.2 %collective-permute-start.16 = (f32[1,8,64]{2,1,0:T(8,128)S(1)}, f32[1,8,64]{2,1,0:T(8,128)S(1)}, u32[]{:S(2)}, u32[]{:S(2)}) collective-permute-start(f32[1,8,64]{2,1,0:T(8,128)S(1)} %collective-permute-done.15), channel_id=1, source_target_pairs={{0,2},{2,4},{4,6},{6,8},{8,10},{10,12},{12,14},{14,16},{16,18},{18... | collective-permute-start | bytes 6152 | tf_op jit(solution)/shard_map/ppermute | solution.py:150
  157.7 7.2 %collective-permute-start.23 = (f32[1,8,64]{2,1,0:T(8,128)S(1)}, f32[1,8,64]{2,1,0:T(8,128)S(1)}, u32[]{:S(2)}, u32[]{:S(2)}) collective-permute-start(f32[1,8,64]{2,1,0:T(8,128)S(1)} %collective-permute-done.22), channel_id=1, source_target_pairs={{2,0},{4,2},{6,4},{8,6},{10,8},{12,10},{14,12},{16,14},{18,16},{20... | collective-permute-start | bytes 6152 | tf_op jit(solution)/shard_map/ppermute | solution.py:152
  164.8 7.2 %collective-permute-start.17 = (f32[1,8,64]{2,1,0:T(8,128)S(1)}, f32[1,8,64]{2,1,0:T(8,128)S(1)}, u32[]{:S(2)}, u32[]{:S(2)}) collective-permute-start(f32[1,8,64]{2,1,0:T(8,128)S(1)} %collective-permute-done.16), channel_id=1, source_target_pairs={{0,2},{2,4},{4,6},{6,8},{8,10},{10,12},{12,14},{14,16},{16,18},{18... | collective-permute-start | bytes 6152 | tf_op jit(solution)/shard_map/ppermute | solution.py:150
  164.9 7.2 %collective-permute-start.24 = (f32[1,8,64]{2,1,0:T(8,128)S(1)}, f32[1,8,64]{2,1,0:T(8,128)S(1)}, u32[]{:S(2)}, u32[]{:S(2)}) collective-permute-start(f32[1,8,64]{2,1,0:T(8,128)S(1)} %collective-permute-done.23), channel_id=1, source_target_pairs={{2,0},{4,2},{6,4},{8,6},{10,8},{12,10},{14,12},{16,14},{18,16},{20... | collective-permute-start | bytes 6152 | tf_op jit(solution)/shard_map/ppermute | solution.py:152
  172.0 7.2 %collective-permute-start.18 = (f32[1,8,64]{2,1,0:T(8,128)S(1)}, f32[1,8,64]{2,1,0:T(8,128)S(1)}, u32[]{:S(2)}, u32[]{:S(2)}) collective-permute-start(f32[1,8,64]{2,1,0:T(8,128)S(1)} %collective-permute-done.17), channel_id=1, source_target_pairs={{0,2},{2,4},{4,6},{6,8},{8,10},{10,12},{12,14},{14,16},{16,18},{18... | collective-permute-start | bytes 6152 | tf_op jit(solution)/shard_map/ppermute | solution.py:150
  172.1 7.2 %collective-permute-start.25 = (f32[1,8,64]{2,1,0:T(8,128)S(1)}, f32[1,8,64]{2,1,0:T(8,128)S(1)}, u32[]{:S(2)}, u32[]{:S(2)}) collective-permute-start(f32[1,8,64]{2,1,0:T(8,128)S(1)} %collective-permute-done.24), channel_id=1, source_target_pairs={{2,0},{4,2},{6,4},{8,6},{10,8},{12,10},{14,12},{16,14},{18,16},{20... | collective-permute-start | bytes 6152 | tf_op jit(solution)/shard_map/ppermute | solution.py:152
  179.2 7.2 %collective-permute-start.19 = (f32[1,8,64]{2,1,0:T(8,128)S(1)}, f32[1,8,64]{2,1,0:T(8,128)S(1)}, u32[]{:S(2)}, u32[]{:S(2)}) collective-permute-start(f32[1,8,64]{2,1,0:T(8,128)S(1)} %collective-permute-done.18), channel_id=1, source_target_pairs={{0,2},{2,4},{4,6},{6,8},{8,10},{10,12},{12,14},{14,16},{16,18},{18... | collective-permute-start | bytes 6152 | tf_op jit(solution)/shard_map/ppermute | solution.py:150
  179.3 7.2 %collective-permute-start.26 = (f32[1,8,64]{2,1,0:T(8,128)S(1)}, f32[1,8,64]{2,1,0:T(8,128)S(1)}, u32[]{:S(2)}, u32[]{:S(2)}) collective-permute-start(f32[1,8,64]{2,1,0:T(8,128)S(1)} %collective-permute-done.25), channel_id=1, source_target_pairs={{2,0},{4,2},{6,4},{8,6},{10,8},{12,10},{14,12},{16,14},{18,16},{20... | collective-permute-start | bytes 6152 | tf_op jit(solution)/shard_map/ppermute | solution.py:152
  186.4 7.2 %collective-permute-start.20 = (f32[1,8,64]{2,1,0:T(8,128)S(1)}, f32[1,8,64]{2,1,0:T(8,128)S(1)}, u32[]{:S(2)}, u32[]{:S(2)}) collective-permute-start(f32[1,8,64]{2,1,0:T(8,128)S(1)} %collective-permute-done.19), channel_id=1, source_target_pairs={{0,2},{2,4},{4,6},{6,8},{8,10},{10,12},{12,14},{14,16},{16,18},{18... | collective-permute-start | bytes 6152 | tf_op jit(solution)/shard_map/ppermute | solution.py:150
  186.5 7.2 %collective-permute-start.27 = (f32[1,8,64]{2,1,0:T(8,128)S(1)}, f32[1,8,64]{2,1,0:T(8,128)S(1)}, u32[]{:S(2)}, u32[]{:S(2)}) collective-permute-start(f32[1,8,64]{2,1,0:T(8,128)S(1)} %collective-permute-done.26), channel_id=1, source_target_pairs={{2,0},{4,2},{6,4},{8,6},{10,8},{12,10},{14,12},{16,14},{18,16},{20... | collective-permute-start | bytes 6152 | tf_op jit(solution)/shard_map/ppermute | solution.py:152
  193.6 7.2 %collective-permute-start.21 = (f32[1,8,64]{2,1,0:T(8,128)S(1)}, f32[1,8,64]{2,1,0:T(8,128)S(1)}, u32[]{:S(2)}, u32[]{:S(2)}) collective-permute-start(f32[1,8,64]{2,1,0:T(8,128)S(1)} %collective-permute-done.20), channel_id=1, source_target_pairs={{0,2},{2,4},{4,6},{6,8},{8,10},{10,12},{12,14},{14,16},{16,18},{18... | collective-permute-start | bytes 6152 | tf_op jit(solution)/shard_map/ppermute | solution.py:150
  193.7 7.3 %collective-permute-start.28 = (f32[1,8,64]{2,1,0:T(8,128)S(1)}, f32[1,8,64]{2,1,0:T(8,128)S(1)}, u32[]{:S(2)}, u32[]{:S(2)}) collective-permute-start(f32[1,8,64]{2,1,0:T(8,128)S(1)} %collective-permute-done.27), channel_id=1, source_target_pairs={{2,0},{4,2},{6,4},{8,6},{10,8},{12,10},{14,12},{16,14},{18,16},{20... | collective-permute-start | bytes 6152 | tf_op jit(solution)/shard_map/ppermute | solution.py:152
  201.9 3.1 %collective-permute-start.29 = (f32[2,16,1,32]{3,1,2,0:T(8,128)S(1)}, f32[2,16,1,32]{3,1,2,0:T(8,128)S(1)}, u32[]{:S(2)}, u32[]{:S(2)}) collective-permute-start(f32[2,16,1,32]{3,1,2,0:T(8,128)S(1)} %slice.753), channel_id=1, source_target_pairs={{1,0},{3,2},{5,4},{7,6},{9,8},{11,10},{13,12},{15,14},{17,16},{19,... | collective-permute-start | bytes 12296 | tf_op jit(solution)/shard_map/ppermute | solution.py:41
  205.0 2.9 %collective-permute-start.30 = (f32[2,16,1,32]{3,1,2,0:T(8,128)S(1)}, f32[2,16,1,32]{3,1,2,0:T(8,128)S(1)}, u32[]{:S(2)}, u32[]{:S(2)}) collective-permute-start(f32[2,16,1,32]{3,1,2,0:T(8,128)S(1)} %slice.755), channel_id=1, source_target_pairs={{0,1},{2,3},{4,5},{6,7},{8,9},{10,11},{12,13},{14,15},{16,17},{18,... | collective-permute-start | bytes 12296 | tf_op jit(solution)/shard_map/ppermute | solution.py:41
  208.0 3.1 %collective-permute-start.31 = (f32[2,16,1,32]{3,1,2,0:T(8,128)S(1)}, f32[2,16,1,32]{3,1,2,0:T(8,128)S(1)}, u32[]{:S(2)}, u32[]{:S(2)}) collective-permute-start(f32[2,16,1,32]{3,1,2,0:T(8,128)S(1)} %slice.759), channel_id=1, source_target_pairs={{1,0},{3,2},{5,4},{7,6},{9,8},{11,10},{13,12},{15,14},{17,16},{19,... | collective-permute-start | bytes 12296 | tf_op jit(solution)/shard_map/ppermute | solution.py:41
  211.1 4.3 %collective-permute-start.32 = (f32[2,16,1,32]{3,1,2,0:T(8,128)S(1)}, f32[2,16,1,32]{3,1,2,0:T(8,128)S(1)}, u32[]{:S(2)}, u32[]{:S(2)}) collective-permute-start(f32[2,16,1,32]{3,1,2,0:T(8,128)S(1)} %slice.761), channel_id=1, source_target_pairs={{0,1},{2,3},{4,5},{6,7},{8,9},{10,11},{12,13},{14,15},{16,17},{18,... | collective-permute-start | bytes 12296 | tf_op jit(solution)/shard_map/ppermute | solution.py:41
